TPU v7x, 32 devices: a whole 2x2x4 slice. The times are simulated.
32 devices in a mesh: nodes: 8 (over z, x), feat: 4 (over y, core).
Axes of the slice: x: 2, y: 2, z: 4, core: 2. Of those that a mesh axis runs over, the one named last changes fastest.
Arguments:
- features: bfloat16 [128, 32768], P('feat', 'nodes'), may hold values from -6 to 6
- w_self: bfloat16 [128, 256], replicated, may hold values from -0.5 to 0.5
- w_neigh: bfloat16 [128, 256], replicated, may hold values from -0.5 to 0.5
- hidden_bias: float32 [256], replicated, may hold values from -3 to 3
- cotangent: bfloat16 [256, 32768], P('feat', 'nodes'), may hold values from -0.032958984 to 0.032958984
- hub_local: int32 [8, 32], P('nodes'), may hold values from 0 to 4095
- send_rows: int32 [8, 8, 128], P('nodes'), may hold values from 0 to 4095
- send_count: int32 [8, 8], P('nodes'), may hold values from 0 to 128, as said below
- tile_values: bfloat16 [1024, 128, 128], P('nodes'), may hold values from 0 to 0.039794922
- tile_target: int32 [8, 128], P('nodes'), may hold values from 0 to 31, as said below
- tile_anchor: int32 [8, 128], P('nodes'), may hold values from 0 to 41, as said below
- tile_count: int32 [8], P('nodes'), may hold values from 42 to 128, as said below
Outputs:
- hidden: bfloat16 [256, 32768], P('feat', 'nodes')
- grad_self: float32 [128, 256], P(None, 'feat')
- grad_neigh: float32 [128, 256], P(None, 'feat')
- bias_grad: float32 [256], P('feat')
Inputs may be any that keep to these rules, and one draw needn't show every extreme that they name: hub_local[q, j] is the local row of partition q's j-th hub node; hubs are ordered by owner, then by j. send_rows[q, p, j] is the local row of partition q that fills slot j of what q sends to p; slots at or after send_count[q, p] are padding. `send_count`: A partition sends nothing to itself, and every partition fills all 128 slots for at least one other partition. `tile_target`: A block is 128 consecutive local nodes. On every partition each block is the destination of some live tile. `tile_anchor`: A block is 128 consecutive rows of source_p. On every partition each source block that holds halo or hub rows is used by some live tile. Tile slots at or after tile_count[p] are padding: their tile_values, tile_target and tile_anchor entries are arbitrary and must be ignored. Some partition fills all 128 slots.
All inputs are finite; a program needn't handle non-finite values.
Results may differ from a plain program's by a relative error of at most 0.0055.
Values may be sent and summed in bfloat16 or wider, within the bound.
No kernel may reach another device: no remote copies, remote signals or barrier semaphores. Data moves between devices by JAX's collectives and lax.ppermute only.
A program may use at most 64 MiB of HBM per device.

v0:
```python
import jax
import jax.numpy as jnp
from jax import lax
from jax.sharding import PartitionSpec as P

TSTEP = 32


def local(
    features,
    w_self,
    w_neigh,
    hidden_bias,
    cotangent,
    hub_local,
    send_rows,
    send_count,
    tile_values,
    tile_target,
    tile_anchor,
    tile_count,
):
    node_parts = lax.axis_size("nodes")
    feat_parts = lax.axis_size("feat")
    feat_index = lax.axis_index("feat")
    width_local, node_local = features.shape
    slot_count = send_rows.shape[2]
    hub_count = hub_local.shape[1]
    tile_size = tile_values.shape[1]
    hidden_local = w_self.shape[1] // feat_parts
    own_hubs = jnp.take(features, hub_local[0], axis=1)
    outgoing = jnp.take(features, send_rows[0].reshape(-1), axis=1).reshape(
        width_local, node_parts, slot_count
    )
    live_slot = (
        lax.broadcasted_iota(jnp.int32, (node_parts, slot_count), 1) < send_count[0][:, None]
    )
    outgoing = jnp.where(live_slot[None], outgoing, jnp.zeros_like(outgoing))
    copies = jnp.broadcast_to(own_hubs[:, None, :], (width_local, node_parts, hub_count))
    halo_rows, hub_parts = (
        lax.all_to_all(outgoing, "nodes", split_axis=1, concat_axis=1, tiled=True),
        lax.all_to_all(copies, "nodes", split_axis=1, concat_axis=1, tiled=True),
    )
    hub_rows = hub_parts.reshape(width_local, node_parts * hub_count)
    source_rows = jnp.concatenate(
        [features, halo_rows.reshape(width_local, node_parts * slot_count), hub_rows], axis=1
    )
    source_blocks = source_rows.reshape(width_local, -1, tile_size)
    local_blocks = node_local // tile_size
    live_count = tile_count[0]
    turns = (live_count + TSTEP - 1) // TSTEP
    block_ids = jnp.arange(local_blocks, dtype=jnp.int32)

    def one_turn(turn_index, running):
        first_tile = turn_index * TSTEP
        tile_block = lax.dynamic_slice_in_dim(tile_values, first_tile, TSTEP, 0)
        targets = lax.dynamic_slice_in_dim(tile_target[0], first_tile, TSTEP, 0)
        anchors = lax.dynamic_slice_in_dim(tile_anchor[0], first_tile, TSTEP, 0)
        live_tiles = first_tile + jnp.arange(TSTEP, dtype=jnp.int32) < live_count
        picked = jnp.take(source_blocks, anchors, axis=1)
        products = jnp.einsum(
            "ftk,tik->fti", picked, tile_block, preferred_element_type=jnp.float32
        )
        selector = ((targets[:, None] == block_ids[None, :]) & live_tiles[:, None]).astype(
            jnp.float32
        )
        return running + jnp.einsum(
            "fti,tn->fni", products, selector, precision=lax.Precision.HIGHEST
        )

    empty = jnp.zeros((width_local, local_blocks, tile_size), jnp.float32)
    aggregate = (
        lax.fori_loop(0, turns, one_turn, empty)
        .reshape(width_local, node_local)
        .astype(jnp.bfloat16)
    )
    contract_first = (((0,), (0,)), ((), ()))
    contract_last = (((1,), (1,)), ((), ()))
    full_inputs, full_aggregate = (
        lax.all_gather(features, "feat", axis=0, tiled=True),
        lax.all_gather(aggregate, "feat", axis=0, tiled=True),
    )
    self_cols = lax.dynamic_slice_in_dim(w_self, feat_index * hidden_local, hidden_local, 1)
    neigh_cols = lax.dynamic_slice_in_dim(w_neigh, feat_index * hidden_local, hidden_local, 1)
    preact = lax.dot_general(
        self_cols, full_inputs, contract_first, preferred_element_type=jnp.float32
    )
    preact = preact + lax.dot_general(
        neigh_cols, full_aggregate, contract_first, preferred_element_type=jnp.float32
    )
    bias_local = lax.dynamic_slice_in_dim(hidden_bias, feat_index * hidden_local, hidden_local, 0)
    preact = preact + bias_local[:, None]
    sigmoid_value = jax.nn.sigmoid(preact)
    hidden = (preact * sigmoid_value).astype(jnp.bfloat16)
    pre_grad = (
        cotangent.astype(jnp.float32) * sigmoid_value * (1.0 + preact * (1.0 - sigmoid_value))
    ).astype(jnp.bfloat16)
    bias_part = jnp.sum(pre_grad, axis=1, dtype=jnp.float32)
    own_grad = lax.dot_general(
        full_inputs, pre_grad, contract_last, preferred_element_type=jnp.float32
    )
    neigh_grad = lax.dot_general(
        full_aggregate, pre_grad, contract_last, preferred_element_type=jnp.float32
    )
    weight_part = jnp.stack([own_grad, neigh_grad])
    weight_total, bias_grad = lax.psum((weight_part, bias_part), "nodes")
    return (hidden, weight_total[0], weight_total[1], bias_grad)


def solution(mesh):
    in_specs = (
        P("feat", "nodes"),
        P(),
        P(),
        P(),
        P("feat", "nodes"),
        P("nodes", None),
        P("nodes", None, None),
        P("nodes", None),
        P("nodes", None, None),
        P("nodes", None),
        P("nodes", None),
        P("nodes"),
    )
    out_specs = (P("feat", "nodes"), P(None, "feat"), P(None, "feat"), P("feat"))
    return jax.shard_map(local, mesh=mesh, in_specs=in_specs, out_specs=out_specs, check_vma=False)
```

profile of v0, /device:TPU:0, one launch (start us, length us, event | category | flops | bytes accessed | tf_op | source)
XLA Modules:
  0.0 152.6 jit_solution(10035392069236234365)
XLA Ops:
  8.6 1.4 copy.32
  10.8 0.7 reshape.199
  11.5 7.3 %all-to-all-start.1 = ((bf16[8,2,512]{2,1,0:T(2,128)(2,1)}), bf16[8,2,512]{2,1,0:T(2,128)(2,1)S(1)}, u32[]{:S(2)}, u32[]{:S(2)}) async-start(bf16[8,2,512]{2,1,0:T(2,128)(2,1)} %reshape.199), calls=%async_computation.1 | async-start | bytes 32768 | tf_op jit(solution)/shard_map/all_to_all | solution.py:42
  18.8 0.8 iota_compare_fusion.1
  20.3 3.2 %gather_fusion.1 = bf16[1024,32]{1,0:T(8,128)(2,1)S(1)} fusion(bf16[32,4096]{0,1:T(8,128)(2,1)S(1)} %copy.32, s32[1024]{0:T(1024)S(1)} %broadcast_clamp_fusion), kind=kCustom, calls=%fused_computation.1 | custom fusion | bytes 135168 | tf_op jit(solution)/shard_map/jit(_take)/gather | solution.py:32
  24.3 1.1 all-to-all-done.1
  25.4 4.9 %all-to-all-start = ((bf16[32,8,128]{2,0,1:T(8,128)(2,1)}), bf16[32,8,128]{2,0,1:T(8,128)(2,1)S(1)}, u32[]{:S(2)}, u32[]{:S(2)}) async-start(bf16[32,8,128]{2,0,1:T(8,128)(2,1)} %select_select_fusion), calls=%async_computation | async-start | bytes 131072 | tf_op jit(solution)/shard_map/all_to_all | solution.py:41
  32.0 5.2 %all-to-all-done = bf16[32,8,128]{2,0,1:T(8,128)(2,1)S(1)} async-done(((bf16[32,8,128]{2,0,1:T(8,128)(2,1)}), bf16[32,8,128]{2,0,1:T(8,128)(2,1)S(1)}, u32[]{:S(2)}, u32[]{:S(2)}) %all-to-all-start) | async-done | bytes 65568 | tf_op jit(solution)/shard_map/all_to_all | solution.py:41
  37.2 1.0 copy_bitcast_fusion
  38.3 8.6 %while.11 = (s32[]{:T(128)}, f32[32,32,128]{2,1,0:T(8,128)S(1)}, s32[]{:T(128)}, s32[1,128]{1,0:T(1,128)S(1)}, s32[]{:T(128)}, /*index=5*/bf16[128,128,128]{2,1,...) while((s32[]{:T(128)}, f32[32,32,128]{2,1,0:T(8,128)S(1)}, ...), condition=%wide.region_1.2_spmd.clone, body=%wide.region_0.1_spmd.clone.sunk | while | flops 84151648 | bytes 3937595 | solution.py:73
  38.5 0.7 compare_and_fusion.4
  39.8 2.0 %convolution_bitcast_fusion.5 = f32[32,32,128]{2,0,1:T(8,128)S(1)} fusion(bf16[128,128,128]{2,1,0:T(8,128)(2,1)} %get-tuple-element.204, s32[]{:T(128)S(6)} %select_n.130, bf16[32,32,128]{2,1,0:T(8,128)(2,1)S(1)} %gather_fusion, pred[32]{0:T(512)(128)(4,1)S(1)} %get-tuple-element.173), kind=kOutput, calls=%fused_computation.5.clone.1 | convolution fusion | flops 33685504 | bytes 1835044 | tf_op jit(solution)/shard_map/while/body/ftk,tik->fti/dot_general | solution.py:61
  41.8 0.8 fusion.45
  42.8 0.7 compare_and_fusion.4
  44.1 1.9 %convolution_bitcast_fusion.5 = f32[32,32,128]{2,0,1:T(8,128)S(1)} fusion(bf16[128,128,128]{2,1,0:T(8,128)(2,1)} %get-tuple-element.204, s32[]{:T(128)S(6)} %select_n.130, bf16[32,32,128]{2,1,0:T(8,128)(2,1)S(1)} %gather_fusion, pred[32]{0:T(512)(128)(4,1)S(1)} %get-tuple-element.173), kind=kOutput, calls=%fused_computation.5.clone.1 | convolution fusion | flops 33685504 | bytes 1835044 | tf_op jit(solution)/shard_map/while/body/ftk,tik->fti/dot_general | solution.py:61
  46.0 0.8 fusion.45
  46.9 0.8 copy.47
  47.9 2.9 %all-gather.3.cloned.1.call-done = bf16[128,4096]{1,0:T(8,128)(2,1)} async-done(((bf16[32,4096]{1,0:T(8,128)(2,1)}), bf16[128,4096]{1,0:T(8,128)(2,1)}) %all-gather.3.cloned.1.call-update) | async-done | bytes 1048592 | tf_op jit(solution)/shard_map/all_gather | solution.py:80
  50.8 1.6 %fusion.20 = f32[64,4096]{1,0:T(8,128)S(1)} fusion(bf16[128,4096]{1,0:T(8,128)(2,1)} %all-gather.3.cloned.1.call-done, bf16[128,256]{1,0:T(8,128)(2,1)S(1)} %copy-done.3, s32[]{:T(128)S(6)} %select_n.85), kind=kOutput, calls=%fused_computation.46 | convolution fusion | flops 67108864 | bytes 2129924 | tf_op jit(solution)/shard_map/dot_general | solution.py:85
  52.4 18.1 %all-gather.5.cloned.1.call-done = bf16[128,4096]{1,0:T(8,128)(2,1)} async-done(((bf16[32,4096]{1,0:T(8,128)(2,1)}), bf16[128,4096]{1,0:T(8,128)(2,1)}) %all-gather.5.cloned.1.call-update) | async-done | bytes 1048592 | tf_op jit(solution)/shard_map/all_gather | solution.py:81
  70.5 3.0 %convert_reduce_fusion = (f32[64]{0:T(128)S(1)}, bf16[64,4096]{1,0:T(8,128)(2,1)S(1)}, bf16[64,4096]{1,0:T(8,128)(2,1)}) fusion(bf16[64,4096]{1,0:T(8,128)(2,1)S(1)} %copy-done.5, f32[64]{0:T(128)S(1)} %dynamic_slice.24, f32[64,4096]{1,0:T(8,128)S(1)} %fusion.20, bf16[128,4096]{1,0:T(8,128)(2,1)} %all-gather.5.cloned.1.call-done, ...), kind=kOutput, calls=%fused_computation.33 | convolution fusion | flops 71303104 | bytes 3703556 | tf_op jit(solution)/shard_map/dot_general | solution.py:88
  75.2 21.9 %psum.15 = f32[64]{0:T(128)} all-reduce(f32[64]{0:T(128)S(1)} %get-tuple-element.112), channel_id=1, replica_groups=mesh['nodes'=8,'feat'=4] {'nodes'}, use_global_device_ids=true, to_apply=%region_4.5 | all-reduce | flops 64 | bytes 512 | tf_op jit(solution)/shard_map/psum | solution.py:106
  97.0 47.6 %all-reduce.2.cloned.1.call-done = f32[2,128,64]{1,2,0:T(8,128)} async-done(((f32[2,128,64]{1,2,0:T(8,128)}), f32[2,128,64]{1,2,0:T(8,128)}) %all-reduce.2.cloned.1.call-update) | async-done | bytes 65552 | tf_op jit(solution)/shard_map/psum | solution.py:106
  144.6 1.4 slice_bitcast_fusion
  (51 shorter events, 8.0 us)
Async XLA Ops:
  7.2 63.4 %copy-start = (bf16[128,256]{1,0:T(8,128)(2,1)S(1)}, bf16[128,256]{1,0:T(8,128)(2,1)}, u32[]{:S(2)}) copy-start(bf16[128,256]{1,0:T(8,128)(2,1)} %param.16) | copy-start | bytes 196612
  7.2 31.1 %copy-start.4 = (s32[1,128]{1,0:T(1,128)S(1)}, s32[1,128]{1,0:T(1,128)}, u32[]{:S(2)}) copy-start(s32[1,128]{1,0:T(1,128)} %param.24) | copy-start | bytes 1540
  7.2 31.1 %copy-start.7 = (s32[1,128]{1,0:T(1,128)S(1)}, s32[1,128]{1,0:T(1,128)}, u32[]{:S(2)}) copy-start(s32[1,128]{1,0:T(1,128)} %param.23) | copy-start | bytes 1540
  11.5 13.9 %all-to-all-start.1 = ((bf16[8,2,512]{2,1,0:T(2,128)(2,1)}), bf16[8,2,512]{2,1,0:T(2,128)(2,1)S(1)}, u32[]{:S(2)}, u32[]{:S(2)}) async-start(bf16[8,2,512]{2,1,0:T(2,128)(2,1)} %reshape.199), calls=%async_computation.1 | async-start | bytes 32768 | tf_op jit(solution)/shard_map/all_to_all | solution.py:42
  25.4 11.8 %all-to-all-start = ((bf16[32,8,128]{2,0,1:T(8,128)(2,1)}), bf16[32,8,128]{2,0,1:T(8,128)(2,1)S(1)}, u32[]{:S(2)}, u32[]{:S(2)}) async-start(bf16[32,8,128]{2,0,1:T(8,128)(2,1)} %select_select_fusion), calls=%async_computation | async-start | bytes 131072 | tf_op jit(solution)/shard_map/all_to_all | solution.py:41
  30.3 20.5 %all-gather.3.cloned.1.call-start = ((), (), s32[]{:S(2)}) async-start(), calls=%async_computation.2 | async-start | bytes 1310720 | tf_op jit(solution)/shard_map/all_gather | solution.py:80
  31.0 39.5 %all-gather.5.cloned.1.call-start = ((), (), s32[]{:S(2)}) async-start(), calls=%async_computation.3 | async-start | bytes 1310720 | tf_op jit(solution)/shard_map/all_gather | solution.py:81
  38.3 9.5 %copy-start.6 = (f32[256]{0:T(256)S(1)}, f32[256]{0:T(256)}, u32[]{:S(2)}) copy-start(f32[256]{0:T(256)} %param.17) | copy-start | bytes 3076
  38.3 12.5 %copy-start.3 = (bf16[128,256]{1,0:T(8,128)(2,1)S(1)}, bf16[128,256]{1,0:T(8,128)(2,1)}, u32[]{:S(2)}) copy-start(bf16[128,256]{1,0:T(8,128)(2,1)} %param.15) | copy-start | bytes 196612
  38.3 32.2 %copy-start.5 = (bf16[64,4096]{1,0:T(8,128)(2,1)S(1)}, bf16[64,4096]{1,0:T(8,128)(2,1)}, u32[]{:S(2)}) copy-start(bf16[64,4096]{1,0:T(8,128)(2,1)} %param.18) | copy-start | bytes 1572868
  47.7 96.9 %all-reduce.2.cloned.1.call-start = ((), (), s32[]{:S(2)}) async-start(), calls=%async_computation.4 | async-start | bytes 131072 | tf_op jit(solution)/shard_map/psum | solution.py:106
  52.4 21.6 %copy-start.1 = (bf16[128,4096]{1,0:T(8,128)(2,1)S(1)}, bf16[128,4096]{1,0:T(8,128)(2,1)}, u32[]{:S(2)}) copy-start(bf16[128,4096]{1,0:T(8,128)(2,1)} %all-gather.3.cloned.1.call-done) | copy-start | bytes 3145732
  70.5 3.0 %copy-start.2 = (bf16[128,4096]{1,0:T(8,128)(2,1)S(1)}, bf16[128,4096]{1,0:T(8,128)(2,1)}, u32[]{:S(2)}) copy-start(bf16[128,4096]{1,0:T(8,128)(2,1)} %all-gather.5.cloned.1.call-done) | copy-start | bytes 3145732
Sparse Core Ops, SparseCore 0:
  32.6 18.1 all-gather.2
  52.9 17.5 all-gather.4
  75.3 69.2 all-reduce.1
where the time goes:
time: 153 us
  waiting for transfers between devices  75.6 us (49%)
  blocking collectives  21.9 us (14%)
  between operations  14.6 us (10%)
  starting transfers between devices  12.3 us (8%)
  matrix products  11.1 us (7%)
  local copies, waits for them, and re-layouts  10.2 us (7%)
  other arithmetic  6.84 us (4%)
    psum x1, waiting for transfers between devices, local(): weight_total, bias_grad = lax.psum((weight_part, bias_part), 'nodes')  47.6 us
    psum x1, blocking collectives, local(): weight_total, bias_grad = lax.psum((weight_part, bias_part), 'nodes')  21.9 us
    all_gather x1, waiting for transfers between devices, local(): lax.all_gather(aggregate, 'feat', axis=0, tiled=True)  18.1 us
    all_to_all x1, starting transfers between devices, local(): lax.all_to_all(copies, 'nodes', split_axis=1, concat_axis=1, tiled=True)  7.28 us
    all_to_all x1, waiting for transfers between devices, local(): lax.all_to_all(outgoing, 'nodes', split_axis=1, concat_axis=1, tiled=True)  5.21 us
    all_to_all x1, starting transfers between devices, local(): lax.all_to_all(outgoing, 'nodes', split_axis=1, concat_axis=1, tiled=True)  4.89 us
    dot_general x2, matrix products, one_turn(): jnp.einsum('ftk,tik->fti', picked, tile_block, preferred_element_type=jnp...  3.87 us
    gather x2, local copies, waits for them, and re-layouts, local(): jnp.take(features, send_rows[0].reshape(-1), axis=1)  3.33 us
  transfers between devices with their start and end apart: 5, of which 5 were waited for; matrix products, arithmetic and copies ran while one was open for 12% of the time, Pallas kernels for 0%

commit v1 on v0

--- a/solution.py
+++ b/solution.py
@@ -4,6 +4,27 @@
 from jax.sharding import PartitionSpec as P
 
 TSTEP = 32
+
+
+def joined_along(blocks, dim):
+    lengths = list(blocks.shape[1:])
+    lengths[dim] *= blocks.shape[0]
+    return jnp.moveaxis(blocks, 0, dim).reshape(lengths)
+
+
+def collected_by_bits(x, axis):
+    size, index = (lax.axis_size(axis), lax.axis_index(axis))
+    blocks, bit = (x[None], 1)
+    while bit < size:
+        other = lax.ppermute(blocks, axis, [(i, i ^ bit) for i in range(size)])
+        low = index & bit == 0
+        blocks = jnp.concatenate([jnp.where(low, blocks, other), jnp.where(low, other, blocks)])
+        bit *= 2
+    return blocks
+
+
+def collect(x, axis, dim):
+    return joined_along(collected_by_bits(x, axis), dim)
 
 
 def local(
@@ -78,7 +99,7 @@
     contract_last = (((1,), (1,)), ((), ()))
     full_inputs, full_aggregate = (
         lax.all_gather(features, "feat", axis=0, tiled=True),
-        lax.all_gather(aggregate, "feat", axis=0, tiled=True),
+        collect(aggregate, "feat", 0),
     )
     self_cols = lax.dynamic_slice_in_dim(w_self, feat_index * hidden_local, hidden_local, 1)
     neigh_cols = lax.dynamic_slice_in_dim(w_neigh, feat_index * hidden_local, hidden_local, 1)

time: 153 us -> 159 us (1.039)
  waiting for transfers between devices: 75.6 us -> 78.9 us
  blocking collectives: 21.9 us -> 24.2 us
  starting transfers between devices: 12.3 us -> 13.9 us
    all_gather x1 -> x0, waiting for transfers between devices: 18.1 us -> none  [local(): lax.all_gather(aggregate, 'feat', axis=0, tiled=True)]
    ppermute x0 -> x2, waiting for transfers between devices: none -> 13.8 us  [collected_by_bits(): other = lax.ppermute(blocks, axis, [(i, i ^ bit) for i in range(size)])]
    all_gather x1, waiting for transfers between devices: 2.9 us -> 9.2 us  [local(): lax.all_gather(features, 'feat', axis=0, tiled=True)]
    psum x1, blocking collectives: 21.9 us -> 24.2 us  [local(): weight_total, bias_grad = lax.psum((weight_part, bias_part), 'nodes')]
    ppermute x0 -> x2, starting transfers between devices: none -> 1.65 us  [collected_by_bits(): other = lax.ppermute(blocks, axis, [(i, i ^ bit) for i in range(size)])]
  transfers between devices with their start and end apart: 5 -> 6, of which waited for: 5 -> 6; matrix products, arithmetic and copies ran while one was open for 12% -> 4% of each run, Pallas kernels for 0% -> 0%
where the time goes in v1:
time: 159 us; the launch traced here: 158 us
  waiting for transfers between devices  78.9 us (50%)
  blocking collectives  24.2 us (15%)
  between operations  15 us (9%)
  starting transfers between devices  13.9 us (9%)
  matrix products  9.78 us (6%)
  local copies, waits for them, and re-layouts  9.46 us (6%)
  other arithmetic  7.09 us (4%)
    psum x1, waiting for transfers between devices, local(): weight_total, bias_grad = lax.psum((weight_part, bias_part), 'nodes')  48.8 us
    psum x1, blocking collectives, local(): weight_total, bias_grad = lax.psum((weight_part, bias_part), 'nodes')  24.2 us
    ppermute x2, waiting for transfers between devices, collected_by_bits(): other = lax.ppermute(blocks, axis, [(i, i ^ bit) for i in range(size)])  13.8 us
    all_gather x1, waiting for transfers between devices, local(): lax.all_gather(features, 'feat', axis=0, tiled=True)  9.2 us
    all_to_all x1, starting transfers between devices, local(): lax.all_to_all(copies, 'nodes', split_axis=1, concat_axis=1, tiled=True)  7.28 us
    all_to_all x1, waiting for transfers between devices, local(): lax.all_to_all(outgoing, 'nodes', split_axis=1, concat_axis=1, tiled=True)  5.94 us
    all_to_all x1, starting transfers between devices, local(): lax.all_to_all(outgoing, 'nodes', split_axis=1, concat_axis=1, tiled=True)  4.89 us
    dot_general x2, matrix products, one_turn(): jnp.einsum('ftk,tik->fti', picked, tile_block, preferred_element_type=jnp...  3.83 us
  transfers between devices with their start and end apart: 6, of which 6 were waited for; matrix products, arithmetic and copies ran while one was open for 4% of the time, Pallas kernels for 0%

profile of v1, /device:TPU:0, one launch (start us, length us, event | category | flops | bytes accessed | tf_op | source)
XLA Modules:
  0.0 158.3 jit_solution(18238799915872073263)
XLA Ops:
  8.6 1.4 copy.32
  10.8 0.7 reshape.213
  11.5 7.3 %all-to-all-start.1 = ((bf16[8,2,512]{2,1,0:T(2,128)(2,1)}), bf16[8,2,512]{2,1,0:T(2,128)(2,1)S(1)}, u32[]{:S(2)}, u32[]{:S(2)}) async-start(bf16[8,2,512]{2,1,0:T(2,128)(2,1)} %reshape.213), calls=%async_computation.1 | async-start | bytes 32768 | tf_op jit(solution)/shard_map/all_to_all | solution.py:63
  18.8 0.8 iota_compare_fusion.1
  20.3 3.2 %gather_fusion.1 = bf16[1024,32]{1,0:T(8,128)(2,1)S(1)} fusion(bf16[32,4096]{0,1:T(8,128)(2,1)S(1)} %copy.32, s32[1024]{0:T(1024)S(1)} %broadcast_clamp_fusion), kind=kCustom, calls=%fused_computation.1 | custom fusion | bytes 135168 | tf_op jit(solution)/shard_map/jit(_take)/gather | solution.py:53
  24.3 1.1 all-to-all-done.1
  25.4 4.9 %all-to-all-start = ((bf16[32,8,128]{2,0,1:T(8,128)(2,1)}), bf16[32,8,128]{2,0,1:T(8,128)(2,1)S(1)}, u32[]{:S(2)}, u32[]{:S(2)}) async-start(bf16[32,8,128]{2,0,1:T(8,128)(2,1)} %select_select_fusion), calls=%async_computation | async-start | bytes 131072 | tf_op jit(solution)/shard_map/all_to_all | solution.py:62
  31.2 5.9 %all-to-all-done = bf16[32,8,128]{2,0,1:T(8,128)(2,1)S(1)} async-done(((bf16[32,8,128]{2,0,1:T(8,128)(2,1)}), bf16[32,8,128]{2,0,1:T(8,128)(2,1)S(1)}, u32[]{:S(2)}, u32[]{:S(2)}) %all-to-all-start) | async-done | bytes 65568 | tf_op jit(solution)/shard_map/all_to_all | solution.py:62
  37.2 1.0 copy_bitcast_fusion
  38.3 8.5 %while.11 = (s32[]{:T(128)}, f32[32,32,128]{2,1,0:T(8,128)S(1)}, s32[]{:T(128)}, s32[1,128]{1,0:T(1,128)S(1)}, s32[]{:T(128)}, /*index=5*/bf16[128,128,128]{2,1,...) while((s32[]{:T(128)}, f32[32,32,128]{2,1,0:T(8,128)S(1)}, ...), condition=%wide.region_1.2_spmd.clone, body=%wide.region_0.1_spmd.clone.sunk | while | flops 84151648 | bytes 3937595 | solution.py:94
  39.8 1.9 %convolution_bitcast_fusion.5 = f32[32,32,128]{2,0,1:T(8,128)S(1)} fusion(bf16[128,128,128]{2,1,0:T(8,128)(2,1)} %get-tuple-element.208, s32[]{:T(128)S(6)} %select_n.168, bf16[32,32,128]{2,1,0:T(8,128)(2,1)S(1)} %gather_fusion, pred[32]{0:T(512)(128)(4,1)S(1)} %get-tuple-element.177), kind=kOutput, calls=%fused_computation.5.clone.1 | convolution fusion | flops 33685504 | bytes 1835044 | tf_op jit(solution)/shard_map/while/body/ftk,tik->fti/dot_general | solution.py:82
  41.7 0.8 fusion.45
  42.7 0.7 compare_and_fusion.4
  44.0 1.9 %convolution_bitcast_fusion.5 = f32[32,32,128]{2,0,1:T(8,128)S(1)} fusion(bf16[128,128,128]{2,1,0:T(8,128)(2,1)} %get-tuple-element.208, s32[]{:T(128)S(6)} %select_n.168, bf16[32,32,128]{2,1,0:T(8,128)(2,1)S(1)} %gather_fusion, pred[32]{0:T(512)(128)(4,1)S(1)} %get-tuple-element.177), kind=kOutput, calls=%fused_computation.5.clone.1 | convolution fusion | flops 33685504 | bytes 1835044 | tf_op jit(solution)/shard_map/while/body/ftk,tik->fti/dot_general | solution.py:82
  46.0 0.8 fusion.45
  47.1 1.5 collective-permute-done
  48.7 1.6 collective-permute-start.1
  50.4 12.3 %collective-permute-done.1 = bf16[2,32,4096]{2,1,0:T(8,128)(2,1)S(1)} collective-permute-done((bf16[2,32,4096]{2,1,0:T(8,128)(2,1)S(1)}, bf16[2,32,4096]{2,1,0:T(8,128)(2,1)S(1)}, u32[]{:S(2)}, u32[]{:S(2)}) %collective-permute-start.1) | collective-permute-done | bytes 524320 | tf_op jit(solution)/shard_map/ppermute | solution.py:19
  62.9 9.2 %all-gather.2.cloned.1.call-done = bf16[128,4096]{1,0:T(8,128)(2,1)} async-done(((bf16[32,4096]{1,0:T(8,128)(2,1)}), bf16[128,4096]{1,0:T(8,128)(2,1)}) %all-gather.2.cloned.1.call-update) | async-done | bytes 1048592 | tf_op jit(solution)/shard_map/all_gather | solution.py:101
  72.1 1.6 %fusion.20 = f32[64,4096]{1,0:T(8,128)S(1)} fusion(bf16[128,4096]{1,0:T(8,128)(2,1)} %all-gather.2.cloned.1.call-done, bf16[128,256]{1,0:T(8,128)(2,1)S(1)} %copy-done.2, s32[]{:T(128)S(6)} %select_n.109), kind=kOutput, calls=%fused_computation.51 | convolution fusion | flops 67108864 | bytes 2129924 | tf_op jit(solution)/shard_map/dot_general | solution.py:106
  73.8 1.7 %convert_reduce_fusion = (f32[64]{0:T(128)S(1)}, bf16[64,4096]{1,0:T(8,128)(2,1)S(1)}, bf16[64,4096]{1,0:T(8,128)(2,1)}) fusion(bf16[64,4096]{1,0:T(8,128)(2,1)S(1)} %copy-done.4, f32[64]{0:T(128)S(1)} %dynamic_slice.24, f32[64,4096]{1,0:T(8,128)S(1)} %fusion.20, bf16[128,4096]{1,0:T(8,128)(2,1)S(1)} %bitcast.86, bf16[128,256]{1,0:T(8,128)(2,1)S(1)} %copy-done, ...), kind=kOutput, calls=%fused_computation.34 | convolution fusion | flops 71303104 | bytes 3703556 | tf_op jit(solution)/shard_map/dot_general | solution.py:109
  77.1 24.2 %psum.15 = f32[64]{0:T(128)} all-reduce(f32[64]{0:T(128)S(1)} %get-tuple-element.112), channel_id=1, replica_groups=mesh['nodes'=8,'feat'=4] {'nodes'}, use_global_device_ids=true, to_apply=%region_4.5 | all-reduce | flops 64 | bytes 512 | tf_op jit(solution)/shard_map/psum | solution.py:127
  101.3 48.8 %all-reduce.2.cloned.1.call-done = f32[2,128,64]{1,2,0:T(8,128)} async-done(((f32[2,128,64]{1,2,0:T(8,128)}), f32[2,128,64]{1,2,0:T(8,128)}) %all-reduce.2.cloned.1.call-update) | async-done | bytes 65552 | tf_op jit(solution)/shard_map/psum | solution.py:127
  150.1 1.4 slice_bitcast_fusion
  (54 shorter events, 8.4 us)
Async XLA Ops:
  7.2 66.6 %copy-start = (bf16[128,256]{1,0:T(8,128)(2,1)S(1)}, bf16[128,256]{1,0:T(8,128)(2,1)}, u32[]{:S(2)}) copy-start(bf16[128,256]{1,0:T(8,128)(2,1)} %param.16) | copy-start | bytes 196612
  7.2 31.1 %copy-start.3 = (s32[1,128]{1,0:T(1,128)S(1)}, s32[1,128]{1,0:T(1,128)}, u32[]{:S(2)}) copy-start(s32[1,128]{1,0:T(1,128)} %param.24) | copy-start | bytes 1540
  7.2 31.1 %copy-start.6 = (s32[1,128]{1,0:T(1,128)S(1)}, s32[1,128]{1,0:T(1,128)}, u32[]{:S(2)}) copy-start(s32[1,128]{1,0:T(1,128)} %param.23) | copy-start | bytes 1540
  11.5 13.9 %all-to-all-start.1 = ((bf16[8,2,512]{2,1,0:T(2,128)(2,1)}), bf16[8,2,512]{2,1,0:T(2,128)(2,1)S(1)}, u32[]{:S(2)}, u32[]{:S(2)}) async-start(bf16[8,2,512]{2,1,0:T(2,128)(2,1)} %reshape.213), calls=%async_computation.1 | async-start | bytes 32768 | tf_op jit(solution)/shard_map/all_to_all | solution.py:63
  25.4 11.8 %all-to-all-start = ((bf16[32,8,128]{2,0,1:T(8,128)(2,1)}), bf16[32,8,128]{2,0,1:T(8,128)(2,1)S(1)}, u32[]{:S(2)}, u32[]{:S(2)}) async-start(bf16[32,8,128]{2,0,1:T(8,128)(2,1)} %select_select_fusion), calls=%async_computation | async-start | bytes 131072 | tf_op jit(solution)/shard_map/all_to_all | solution.py:62
  30.3 41.8 %all-gather.2.cloned.1.call-start = ((), (), s32[]{:S(2)}) async-start(), calls=%async_computation.2 | async-start | bytes 1310720 | tf_op jit(solution)/shard_map/all_gather | solution.py:101
  38.3 12.1 %copy-start.5 = (f32[256]{0:T(256)S(1)}, f32[256]{0:T(256)}, u32[]{:S(2)}) copy-start(f32[256]{0:T(256)} %param.17) | copy-start | bytes 3076
  46.8 25.3 %copy-start.2 = (bf16[128,256]{1,0:T(8,128)(2,1)S(1)}, bf16[128,256]{1,0:T(8,128)(2,1)}, u32[]{:S(2)}) copy-start(bf16[128,256]{1,0:T(8,128)(2,1)} %param.15) | copy-start | bytes 196612
  47.0 1.6 %collective-permute-start = (bf16[1,32,4096]{2,1,0:T(8,128)(2,1)S(1)}, bf16[1,32,4096]{2,1,0:T(8,128)(2,1)S(1)}, u32[]{:S(2)}, u32[]{:S(2)}) collective-permute-start(bf16[1,32,4096]{2,1,0:T(8,128)(2,1)S(1)} %convert_element_type.27), channel_id=1, source_target_pairs={{0,1},{1,0},{2,3},{3,2},{4,5},{5,4},{6,7},{7,6},{8,9},{9,8},{10,11... | collective-permute-start | bytes 786440 | tf_op jit(solution)/shard_map/ppermute | solution.py:19
  47.1 26.7 %copy-start.4 = (bf16[64,4096]{1,0:T(8,128)(2,1)S(1)}, bf16[64,4096]{1,0:T(8,128)(2,1)}, u32[]{:S(2)}) copy-start(bf16[64,4096]{1,0:T(8,128)(2,1)} %param.18) | copy-start | bytes 1572868
  48.7 14.0 %collective-permute-start.1 = (bf16[2,32,4096]{2,1,0:T(8,128)(2,1)S(1)}, bf16[2,32,4096]{2,1,0:T(8,128)(2,1)S(1)}, u32[]{:S(2)}, u32[]{:S(2)}) collective-permute-start(bf16[2,32,4096]{2,1,0:T(8,128)(2,1)S(1)} %pad_maximum_fusion.1), channel_id=1, source_target_pairs={{0,2},{1,3},{2,0},{3,1},{4,6},{5,7},{6,4},{7,5},{8,10},{9,11},{10,... | collective-permute-start | bytes 1572872 | tf_op jit(solution)/shard_map/ppermute | solution.py:19
  50.3 99.8 %all-reduce.2.cloned.1.call-start = ((), (), s32[]{:S(2)}) async-start(), calls=%async_computation.3 | async-start | bytes 131072 | tf_op jit(solution)/shard_map/psum | solution.py:127
  73.8 2.2 %copy-start.1 = (bf16[128,4096]{1,0:T(8,128)(2,1)S(1)}, bf16[128,4096]{1,0:T(8,128)(2,1)}, u32[]{:S(2)}) copy-start(bf16[128,4096]{1,0:T(8,128)(2,1)} %all-gather.2.cloned.1.call-done) | copy-start | bytes 3145732
Sparse Core Ops, SparseCore 0:
  50.4 21.6 all-gather.1
  77.2 72.7 all-reduce.1
